TPU v7x, 32 devices: a whole 2x2x4 slice. The times are simulated.
32 devices in a mesh: boson: 8 (over z, x), block: 4 (over y, core).
Axes of the slice: x: 2, y: 2, z: 4, core: 2. Of those that a mesh axis runs over, the one named last changes fastest.
Arguments:
- gamma_ph: bfloat16 [32, 1024, 1024], P('boson', 'block'), may hold values from -6 to 6
- full_ph: bfloat16 [32, 1024, 1024], P('boson', 'block'), may hold values from -0.1875 to 0.1875
- chi_ph: float32 [32, 1024], P('boson'), may hold values from 0.3 to 3
- pp_vertex: bfloat16 [32, 1024, 1024], P('boson', 'block'), may hold values from -0.1875 to 0.1875
- chi_pp: float32 [32, 1024], P('boson'), may hold values from 0.3 to 3
- relabel: int32 [32, 16, 8], replicated, may hold values from 0 to 31, as said below
Outputs:
- vertex_new: bfloat16 [32, 1024, 1024], P('boson', 'block')
Inputs may be any that keep to these rules, and one draw needn't show every extreme that they name: `relabel`: for each row tile and column block the table is a permutation of the 32 points. The owner of the target point (target // 4) is the source's owner (q // 4) plus a shift modulo 8, and both this shift and the target's position among its owner's points (target % 4) depend only on the row tile, the column block and q % 4. Row tiles b * 4 to (b + 1) * 4 - 1 form row block b; within one row block, at most 17 of the 128 triples of position, row tile and column block share a shift, and some shift is shared by exactly 17; in every row block the shifts 1, 4 and 7 each occur.
All inputs are finite; a program needn't handle non-finite values.
Results may differ from a plain program's by a relative error of at most 0.0063.
Values may be sent and summed in bfloat16 or wider, within the bound.
A program may use at most 128 MiB of HBM per device.

v0:
```python
import functools
import jax
import jax.numpy as jnp
from jax import lax
from jax.experimental import pallas as pl
from jax.experimental.pallas import tpu as pltpu
from jax.sharding import PartitionSpec as P

MESH = pl.DeviceIdType.MESH
DMA = pltpu.SemaphoreType.DMA
PARTS = 4
LANES = 128


def loop(start, stop, body):
    lax.fori_loop(start, stop, lambda i, carry: (body(i), carry)[1], 0)


class Schedule:
    def __init__(self, chunks, capacity, start):
        self.chunks, self.capacity, self.start = chunks, capacity, start
        assert 0 < chunks - start < capacity

    def due(self, g):
        return jnp.maximum(g + 1 - self.start, 0)


class Gather:
    def __init__(self, nblock, shard, whole, sems):
        self.nblock, self.shard, self.whole = nblock, shard, whole
        self.far_s, self.far_r, self.near_s, self.near_r, self.fwd_s, self.fwd_r, self.loc = sems
        self.points, self.rows, order = shard.shape
        self.cols = order // PARTS
        self.chunks = self.points * PARTS
        self.boson = lax.axis_index("boson")
        self.here = lax.axis_index("block")
        self.partner = self.here + 1 - 2 * (self.here % 2)

    def peers(self):
        out = [self.partner]
        for j in range(1, self.nblock // 2):
            out.append((self.here + 2 * j) % self.nblock)
        return out

    def columns(self, g):
        return pl.ds(pl.multiple_of(g % PARTS * self.cols, self.cols), self.cols)

    def source(self, g):
        return self.shard.at[g // PARTS, :, self.columns(g)]

    def place(self, g, owner):
        rows = pl.ds(pl.multiple_of(owner * self.rows, self.rows), self.rows)
        return self.whole.at[g // PARTS, rows, self.columns(g)]

    def far(self, g, j, owner):
        return pltpu.make_async_remote_copy(
            src_ref=self.source(g), dst_ref=self.place(g, owner),
            send_sem=self.far_s.at[j - 1, g], recv_sem=self.far_r.at[j - 1, g],
            device_id=(self.boson, (self.here + 2 * j) % self.nblock), device_id_type=MESH)

    def near(self, g, owner):
        return pltpu.make_async_remote_copy(
            src_ref=self.source(g), dst_ref=self.place(g, owner),
            send_sem=self.near_s.at[g], recv_sem=self.near_r.at[g],
            device_id=(self.boson, self.partner), device_id_type=MESH)

    def forward(self, g, j, owner):
        return pltpu.make_async_remote_copy(
            src_ref=self.place(g, owner), dst_ref=self.place(g, owner),
            send_sem=self.fwd_s.at[j - 1, g], recv_sem=self.fwd_r.at[j - 1, g],
            device_id=(self.boson, self.partner), device_id_type=MESH)

    def own(self):
        rows = pl.ds(pl.multiple_of(self.here * self.rows, self.rows), self.rows)
        return pltpu.make_async_copy(self.shard, self.whole.at[:, rows], self.loc)

    def each_far(self, act):
        for j in range(1, self.nblock // 2):
            act(j)

    def start(self):
        def one(g):
            self.each_far(lambda j: self.far(g, j, self.here).start())
            self.near(g, self.here).start()
        loop(0, self.chunks, one)

    def relay(self, g):
        def one(j):
            owner = (self.here + self.nblock - 2 * j) % self.nblock
            self.far(g, j, owner).wait_recv()
            self.forward(g, j, owner).start()
        self.each_far(one)

    def arrived(self, g):
        self.near(g, self.partner).wait_recv()
        def one(j):
            twin = (self.partner + self.nblock - 2 * j) % self.nblock
            self.forward(g, j, twin).wait_recv()
        self.each_far(one)

    def sent_far(self):
        loop(0, self.chunks,
             lambda g: self.each_far(lambda j: self.far(g, j, self.here).wait_send()))

    def sent_near(self):
        def one(g):
            self.near(g, self.here).wait_send()
            def fwd(j):
                owner = (self.here + self.nblock - 2 * j) % self.nblock
                self.forward(g, j, owner).wait_send()
            self.each_far(fwd)
        loop(0, self.chunks, one)


def gather_scratch(nblock, points):
    far, chunks = max(nblock // 2 - 1, 1), points * PARTS
    return [DMA((far, chunks)), DMA((far, chunks)), DMA((chunks,)), DMA((chunks,)),
            DMA((far, chunks)), DMA((far, chunks)), DMA]


class Exchange:
    def __init__(self, nboson, outgoing, incoming, send, recv):
        self.n, self.outgoing, self.incoming = nboson, outgoing, incoming
        self.send, self.recv = send, recv
        self.capacity = outgoing.shape[1]
        self.boson = lax.axis_index("boson")
        self.block = lax.axis_index("block")

    def peers(self):
        return [(self.boson + s) % self.n for s in range(1, self.n)]

    def shift(self, i):
        return self.n // 2 + (1 - 2 * (i % 2)) * ((i + 1) // 2)

    def copy(self, s, slot, start=0, size=None):
        dest = (self.boson + s) % self.n
        slots = pl.ds(start, self.capacity if size is None else size)
        return pltpu.make_async_remote_copy(
            src_ref=self.outgoing.at[dest, slots], dst_ref=self.incoming.at[slot, slots],
            send_sem=self.send.at[s], recv_sem=self.recv.at[s],
            device_id=(dest, self.block), device_id_type=MESH)

    def pack(self, target, dest, tiles, table, start, size):
        for k in range(size):
            target[dest, start + k] = tiles[table[dest * self.capacity + start + k]]

    def part(self, tiles, table, start, size):
        def pack(i):
            dest = (self.boson + self.shift(i)) % self.n
            self.pack(self.outgoing, dest, tiles, table, start, size)
        def send(i):
            self.copy(self.shift(i), self.boson, start, size).start()
        pack(0)
        def one(i):
            pack(i)
            send(i - 1)
        loop(1, self.n - 1, one)
        return lambda: send(self.n - 2)

    def keep(self, tiles, table):
        self.pack(self.incoming, self.boson, tiles, table, 0, self.capacity)

    def received(self):
        loop(1, self.n, lambda s: self.copy(s, (self.boson + self.n - s) % self.n).wait_recv())

    def sent(self):
        loop(1, self.n, lambda s: self.copy(s, self.boson).wait_send())


def greet(block_peers, boson_peers):
    barrier = pltpu.get_barrier_semaphore()
    boson, block = lax.axis_index("boson"), lax.axis_index("block")
    for peer in block_peers:
        pl.semaphore_signal(barrier, inc=1, device_id=(boson, peer), device_id_type=MESH)
    for peer in boson_peers:
        pl.semaphore_signal(barrier, inc=1, device_id=(peer, block), device_id_type=MESH)
    pl.semaphore_wait(barrier, len(block_peers) + len(boson_peers))


def own_targets(nboson, targets, first_row, row_tiles):
    _, col_blocks, count = targets.shape
    points, per_point = count // nboson, row_tiles * col_blocks
    boson = lax.axis_index("boson")
    flat = targets[pl.ds(first_row, row_tiles)].reshape(per_point, count)
    lane = lax.broadcasted_iota(jnp.int32, flat.shape, 1)
    return jnp.concatenate(
        [jnp.sum(jnp.where(lane == boson * points + q, flat, 0), axis=1, keepdims=True)
         for q in range(points)], axis=0)


def decode(nboson, points, col_blocks, per_point, own):
    total = points * per_point
    boson = lax.axis_index("boson")
    item = lax.broadcasted_iota(jnp.int32, (total, 1), 0)
    shift = ((own >> (points.bit_length() - 1)) - boson) & (nboson - 1)
    target = (own & (points - 1)) * per_point + (item & (per_point - 1))
    def chunk(place):
        wide = col_blocks // PARTS
        column = place & (col_blocks - 1)
        return (place >> (per_point.bit_length() - 1)) * PARTS + (column >> (wide.bit_length() - 1))
    return item, shift, target, chunk(item), chunk(target)


def slot_tables(nboson, capacity, targets, row_tiles, rows):
    _, col_blocks, count = targets.shape
    points, per_point = count // nboson, row_tiles * col_blocks
    total = points * per_point
    boson = lax.axis_index("boson")
    own = own_targets(nboson, targets, lax.axis_index("block") * row_tiles, row_tiles)
    item, shift, target, ahead, home = decode(nboson, points, col_blocks, per_point, own)

    def spread(keys, values, width):
        wanted = lax.broadcasted_iota(jnp.int32, (total, width), 1)
        return jnp.sum(jnp.where(keys == wanted, values, 0), axis=0, keepdims=True)

    same = spread(item, shift, total) == shift
    def rank(key):
        later = same & (spread(item, key, total) > key)
        return capacity - 1 - jnp.sum(jnp.where(later, 1, 0), axis=1, keepdims=True)

    there = ((boson + shift) & (nboson - 1)) * capacity
    here = ((boson - shift) & (nboson - 1)) * capacity
    out_rank, back_rank = rank(ahead * total + item), rank(home * total + target)
    width = rows.shape[0] // 8 * rows.shape[1]
    last_slot, last_item = nboson * capacity - 1, total - 1
    for k, (keys, values, last) in enumerate((
            (item, there + back_rank, last_slot), (there + out_rank, item, last_item),
            (target, here + out_rank, last_slot), (here + back_rank, target, last_item))):
        line = jnp.clip(spread(keys, values, width), 0, last)
        for h in range(width // LANES):
            rows[h * 8 + k:h * 8 + k + 1, :] = line[:, h * LANES:(h + 1) * LANES]


def late_tiles(nboson, targets, row_tiles, schedules):
    row_count, col_blocks, count = targets.shape
    points, per_point = count // nboson, row_tiles * col_blocks
    total, chunks = points * per_point, points * PARTS
    lane = lax.broadcasted_iota(jnp.int32, (total, chunks * nboson), 1)
    wanted, upto = lane & (nboson - 1), lane >> (nboson.bit_length() - 1)
    late = 0
    for b in range(row_count // row_tiles):
        own = own_targets(nboson, targets, b * row_tiles, row_tiles)
        _, shift, _, *arrivals = decode(nboson, points, col_blocks, per_point, own)
        match = shift == wanted
        number = jnp.sum(jnp.where(match, 1, 0), axis=0, keepdims=True)
        for arrival, schedule in zip(arrivals, schedules):
            ready = jnp.sum(jnp.where(match & (arrival <= upto), 1, 0), axis=0, keepdims=True)
            due = schedule.due(upto[0:1]) - (schedule.capacity - number)
            late = late + jnp.where((ready < due) & (wanted[0:1] > 0), 1, 0)
    return jnp.sum(late, axis=1, keepdims=True)


class Table:
    def __init__(self, ref, k):
        self.ref, self.k = ref, k

    def __getitem__(self, i):
        return self.ref[i // LANES * 8 + self.k, i % LANES]


def kernel(nboson, nblock, row_tiles, col_blocks, lag, *refs):
    relabel, gamma_in, full_in, chi_ph, pp_in, chi_pp, out, *refs = refs
    late, refs = (refs[0], refs[1:]) if lag is not None else (None, refs)
    (full, pp, gamma, scaled, base, tiles, packed, landed, back, returned,
     targets, table_rows, table,
     gamma_sem, table_sem, ahead_s, ahead_r, home_s, home_r, *gather_sems) = refs
    half = len(gather_sems) // 2
    first = Gather(nblock, full_in, full, gather_sems[:half])
    second = Gather(nblock, pp_in, pp, gather_sems[half:])
    ahead = Exchange(nboson, packed, landed, ahead_s, ahead_r)
    home = Exchange(nboson, back, returned, home_s, home_r)
    points, rows, order = gamma.shape
    chunks = first.chunks
    high, wide = rows // row_tiles, order // col_blocks
    capacity = landed.shape[1]
    send_slot, item_of, back_slot, back_item_of = (Table(table, i) for i in range(4))
    load_targets = pltpu.make_async_copy(relabel, targets, table_sem.at[0])
    load_table = pltpu.make_async_copy(table_rows, table, table_sem.at[1])
    load_gamma = pltpu.make_async_copy(gamma_in, gamma, gamma_sem)

    first.own().start()
    load_gamma.start()
    load_targets.start()
    second.own().start()
    greet(first.peers(), ahead.peers())
    first.start()

    load_gamma.wait()
    for q in range(points):
        scaled[q] = (gamma[q].astype(jnp.float32) * chi_ph[q:q + 1, :]).astype(jnp.bfloat16)
    load_targets.wait()
    slot_tables(nboson, capacity, targets, row_tiles, table_rows)
    load_table.start()
    if lag is None:
        ahead_plan = home_plan = None
    else:
        ahead_plan = Schedule(chunks, capacity, lag)
        home_plan = Schedule(chunks, capacity, lag)
        late[...] = jnp.broadcast_to(
            late_tiles(nboson, targets, row_tiles, (ahead_plan, home_plan)), late.shape)
    first.own().wait()
    load_table.wait()

    def cut(wire, g):
        q, column = g // PARTS, g % PARTS * (first.cols // wide)
        for r in range(row_tiles):
            for k in range(first.cols // wide):
                item = (q * row_tiles + r) * col_blocks + column + k
                tiles[item] = wire[r * high:(r + 1) * high, k * wide:(k + 1) * wide]

    def product(gather, g):
        q, at = g // PARTS, gather.columns(g)
        phi = jnp.dot(scaled[q], gather.whole[q, :, at], preferred_element_type=jnp.float32)
        cut(phi.astype(jnp.bfloat16), g)
        return q, at, phi

    def ph(g):
        first.arrived(g)
        q, at, phi = product(first, g)
        base[q, :, at] = gamma[q, :, at].astype(jnp.float32) + phi

    def staged(exchange, table, plan, begin, step):
        if plan is None:
            loop(begin, chunks, step)
            sent = 0
        else:
            loop(begin, plan.start, step)
            def one(g):
                step(g)
                exchange.part(tiles, table, g - plan.start, 1)()
            loop(plan.start, chunks, one)
            sent = chunks - plan.start
        last = exchange.part(tiles, table, sent, capacity - sent)
        exchange.keep(tiles, table)
        last()

    def ahead_step(g):
        @pl.when(g + 1 < chunks)
        def _():
            first.relay(g + 1)
        @pl.when(g == chunks - 2)
        def _():
            second.start()
        ph(g)

    first.relay(0)
    staged(ahead, item_of, ahead_plan, 0, ahead_step)
    first.sent_far()
    first.sent_near()
    second.own().wait()
    loop(0, chunks // 2, second.relay)
    ahead.received()

    flat = landed.reshape(nboson * capacity, high, wide)
    def unpack(p):
        chi = chi_pp[pl.ds(p, 1), :]
        for c in range(col_blocks):
            for r in range(row_tiles):
                tile = flat[back_slot[(p * row_tiles + r) * col_blocks + c]]
                scaled[p, r * high:(r + 1) * high, c * wide:(c + 1) * wide] = (
                    tile.astype(jnp.float32) * chi[:, c * wide:(c + 1) * wide]).astype(jnp.bfloat16)

    def home_step(g):
        @pl.when((g + 1 >= chunks // 2) & (g + 1 < chunks))
        def _():
            second.relay(g + 1)
        @pl.when(g % PARTS == 0)
        def _():
            unpack(g // PARTS)
        second.arrived(g)
        product(second, g)

    staged(home, back_item_of, home_plan, 0, home_step)
    ahead.sent()
    second.sent_far()
    second.sent_near()
    home.received()

    flat_back = returned.reshape(nboson * capacity, high, wide)
    def finish(q):
        for r in range(row_tiles):
            for c in range(col_blocks):
                tile = flat_back[send_slot[(q * row_tiles + r) * col_blocks + c]]
                at = (q, slice(r * high, (r + 1) * high), slice(c * wide, (c + 1) * wide))
                out[at] = (base[at] + tile.astype(jnp.float32)).astype(jnp.bfloat16)
    loop(0, points, finish)
    home.sent()


def local(nboson, nblock, gamma_ph, full_ph, chi_ph, pp_vertex, chi_pp, relabel):
    points, rows, order = gamma_ph.shape
    row_tiles, col_blocks = relabel.shape[1] // nblock, relabel.shape[2]
    high, wide = rows // row_tiles, order // col_blocks
    total = points * row_tiles * col_blocks
    capacity = -(-total // nboson) + 1
    bf16, f32 = jnp.bfloat16, jnp.float32
    whole = pltpu.VMEM((points, order, order), bf16)
    shard = pltpu.VMEM(gamma_ph.shape, bf16)
    slabs = pltpu.VMEM((nboson, capacity, high, wide), bf16)
    table_rows = -(-(nboson * capacity) // LANES) * 8
    for count in (nboson, points, row_tiles * col_blocks, col_blocks, PARTS):
        assert count & (count - 1) == 0
    vmem = pl.BlockSpec(memory_space=pltpu.VMEM)
    hbm = pl.BlockSpec(memory_space=pl.ANY)
    operands = (relabel.transpose(1, 2, 0), gamma_ph, full_ph, chi_ph, pp_vertex, chi_pp)

    def window(lag):
        result = pltpu.VMEM(gamma_ph.shape, bf16)
        early = lag is not None
        return pl.pallas_call(
            functools.partial(kernel, nboson, nblock, row_tiles, col_blocks, lag),
            out_shape=(result, pltpu.VMEM((8, LANES), jnp.int32)) if early else result,
            name="early" if early else "plain",
            in_specs=[hbm, hbm, hbm, vmem, hbm, vmem], out_specs=(vmem, vmem) if early else vmem,
            scratch_shapes=[
                whole, whole, shard, shard, pltpu.VMEM(gamma_ph.shape, f32),
                pltpu.VMEM((total, high, wide), bf16), slabs, slabs, slabs, slabs,
                pltpu.VMEM(operands[0].shape, jnp.int32),
                pltpu.VMEM((table_rows, LANES), jnp.int32), pltpu.SMEM((table_rows, LANES), jnp.int32),
                DMA, DMA((2,)), DMA((nboson,)), DMA((nboson,)), DMA((nboson,)), DMA((nboson,)),
            ] + gather_scratch(nblock, points) + gather_scratch(nblock, points),
            compiler_params=pltpu.CompilerParams(
                collective_id=int(early), has_side_effects=True, vmem_limit_bytes=60 * 1024 * 1024),
        )(*operands)

    chunks = points * PARTS
    if capacity <= chunks:
        return window(None)
    result, late = window(LAG * chunks // 16)
    return lax.cond(late[0, 0] == 0, lambda: result, lambda: window(None))


LAG = 6


def solution(mesh):
    placed = (
        P("boson", "block", None),
        P("boson", "block", None),
        P("boson", None),
        P("boson", "block", None),
        P("boson", None),
        P(),
    )
    return jax.shard_map(
        functools.partial(local, mesh.shape["boson"], mesh.shape["block"]), mesh=mesh,
        in_specs=placed, out_specs=P("boson", "block", None), check_vma=False,
    )
```

profile of v0, /device:TPU:10, one launch (start us, length us, event | category | flops | bytes accessed | tf_op | source)
XLA Modules:
  0.0 134.5 jit_solution(10731622698782562190)
XLA Ops:
  0.0 0.0 copy-start
  0.0 0.0 copy-start.1
  0.0 0.0 copy-start.2
  0.0 132.0 %early.1 = (bf16[4,256,1024]{2,1,0:T(8,128)(2,1)S(1)}, s32[8,128]{1,0:T(8,128)S(1)}) custom-call(s32[16,8,32]{2,1,0:T(8,128)} %bitcast.2, bf16[4,256,1024]{2,1,0:T(8,128)(2,1)} %refs_1_.1, bf16[4,256,1024]{2,1,0:T(8,128)(2,1)} %refs_2_.1, f32[4,1024]{1,0:T(4,128)} %refs_3_.1, bf16[4,256,1024]{2,1,0:T(8,128)(2,1)} %refs_4_.1, f32[4,1024]{1,0:T(4,128)} %refs_5_.1), custom_call_target="tpu_custom_call" | custom-call | tf_op jit(solution)/shard_map/early/pallas_call | solution.py:410
  132.0 0.5 slice.3
  133.2 0.0 copy-done
  133.2 0.0 copy-done.1
  133.2 0.0 copy-done.2
  133.2 1.3 copy.12
  (1 shorter events, 0.0 us)
Async XLA Ops:
  0.0 133.2 %copy-start = (s32[32,16,8]{0,2,1:T(8,128)S(1)}, s32[32,16,8]{0,2,1:T(8,128)}, u32[]{:S(2)}) copy-start(s32[32,16,8]{0,2,1:T(8,128)} %param.13) | copy-start | bytes 49156
  0.0 133.2 %copy-start.1 = (f32[4,1024]{1,0:T(4,128)S(1)}, f32[4,1024]{1,0:T(4,128)}, u32[]{:S(2)}) copy-start(f32[4,1024]{1,0:T(4,128)} %refs_3_.1) | copy-start | bytes 49156
  0.0 133.2 %copy-start.2 = (f32[4,1024]{1,0:T(4,128)S(1)}, f32[4,1024]{1,0:T(4,128)}, u32[]{:S(2)}) copy-start(f32[4,1024]{1,0:T(4,128)} %refs_5_.1) | copy-start | bytes 49156
where the time goes:
time: 135 us
  Pallas kernels  132 us (98%)
  local copies, waits for them, and re-layouts  1.85 us (1%)
    pallas_call x1, Pallas kernels, window(): pl.pallas_call(functools.partial(kernel, nboson, nblock, row_tiles, col_b...  132 us

commit v1 on v0

v1 whole, which is shorter than its diff:
```python
import functools
import jax
import jax.numpy as jnp
from jax import lax
from jax.experimental import pallas as pl
from jax.experimental.pallas import tpu as pltpu
from jax.sharding import PartitionSpec as P

MESH = pl.DeviceIdType.MESH
DMA = pltpu.SemaphoreType.DMA
PARTS = 4
FIXED = 2
LAG = 3
LANES = 128


def loop(start, stop, body):
    lax.fori_loop(start, stop, lambda i, carry: (body(i), carry)[1], 0)


class Gather:
    def __init__(self, nblock, shard, blocks, whole, fixed, sems):
        self.nblock, self.shard, self.blocks, self.whole = nblock, shard, blocks, whole
        self.far_s, self.far_r, self.near_s, self.near_r, self.fwd_s, self.fwd_r, self.loc = sems
        self.chunks, _, self.cols = whole.shape
        self.rows = shard.shape[1]
        self.fixed = fixed
        self.boson = lax.axis_index("boson")
        self.here = lax.axis_index("block")
        self.partner = self.here + 1 - 2 * (self.here % 2)

    def peers(self):
        out = [self.partner]
        for j in range(1, self.nblock // 2):
            out.append((self.here + 2 * j) % self.nblock)
        return out

    def place(self, g, owner):
        rows = pl.ds(pl.multiple_of(owner * self.rows, self.rows), self.rows)
        return self.whole.at[g, rows]

    def load(self, g):
        source = self.shard.at[g // PARTS, :, g % PARTS * self.cols:(g % PARTS + 1) * self.cols]
        target = self.place(g, self.here) if g < self.fixed else self.blocks.at[g]
        return pltpu.make_async_copy(source, target, self.loc.at[g])

    def pack(self, order):
        def one(g):
            self.place(g, self.here)[...] = self.blocks[order(g)]
        loop(self.fixed, self.chunks, one)

    def far(self, g, j, owner):
        return pltpu.make_async_remote_copy(
            src_ref=self.place(g, owner), dst_ref=self.place(g, owner),
            send_sem=self.far_s.at[j - 1, g], recv_sem=self.far_r.at[j - 1, g],
            device_id=(self.boson, (self.here + 2 * j) % self.nblock), device_id_type=MESH)

    def near(self, g, owner):
        return pltpu.make_async_remote_copy(
            src_ref=self.place(g, owner), dst_ref=self.place(g, owner),
            send_sem=self.near_s.at[g], recv_sem=self.near_r.at[g],
            device_id=(self.boson, self.partner), device_id_type=MESH)

    def forward(self, g, j, owner):
        return pltpu.make_async_remote_copy(
            src_ref=self.place(g, owner), dst_ref=self.place(g, owner),
            send_sem=self.fwd_s.at[j - 1, g], recv_sem=self.fwd_r.at[j - 1, g],
            device_id=(self.boson, self.partner), device_id_type=MESH)

    def each_far(self, act):
        for j in range(1, self.nblock // 2):
            act(j)

    def start(self, begin, end):
        def one(g):
            self.each_far(lambda j: self.far(g, j, self.here).start())
            self.near(g, self.here).start()
        loop(begin, end, one)

    def relay(self, g):
        def one(j):
            owner = (self.here + self.nblock - 2 * j) % self.nblock
            self.far(g, j, owner).wait_recv()
            self.forward(g, j, owner).start()
        self.each_far(one)

    def arrived(self, g):
        self.near(g, self.partner).wait_recv()
        def one(j):
            twin = (self.partner + self.nblock - 2 * j) % self.nblock
            self.forward(g, j, twin).wait_recv()
        self.each_far(one)

    def sent(self):
        def one(g):
            self.each_far(lambda j: self.far(g, j, self.here).wait_send())
            self.near(g, self.here).wait_send()
            def fwd(j):
                owner = (self.here + self.nblock - 2 * j) % self.nblock
                self.forward(g, j, owner).wait_send()
            self.each_far(fwd)
        loop(0, self.chunks, one)


def gather_scratch(nblock, points):
    far, chunks = max(nblock // 2 - 1, 1), points * PARTS
    return [DMA((far, chunks)), DMA((far, chunks)), DMA((chunks,)), DMA((chunks,)),
            DMA((far, chunks)), DMA((far, chunks)), DMA((chunks,))]


class Exchange:
    def __init__(self, nboson, outgoing, incoming, send, recv):
        self.n, self.outgoing, self.incoming = nboson, outgoing, incoming
        self.send, self.recv = send, recv
        self.capacity = outgoing.shape[1]
        self.boson = lax.axis_index("boson")
        self.block = lax.axis_index("block")

    def peers(self):
        return [(self.boson + s) % self.n for s in range(1, self.n)]

    def shift(self, i):
        return self.n // 2 + (1 - 2 * (i % 2)) * ((i + 1) // 2)

    def copy(self, s, slot, start=0, size=None):
        dest = (self.boson + s) % self.n
        slots = pl.ds(start, self.capacity if size is None else size)
        return pltpu.make_async_remote_copy(
            src_ref=self.outgoing.at[dest, slots], dst_ref=self.incoming.at[slot, slots],
            send_sem=self.send.at[s], recv_sem=self.recv.at[s],
            device_id=(dest, self.block), device_id_type=MESH)

    def pack(self, target, dest, tiles, table, start, size):
        for k in range(size):
            target[dest, start + k] = tiles[table[dest * self.capacity + start + k]]

    def part(self, tiles, table, start, size):
        def pack(i):
            dest = (self.boson + self.shift(i)) % self.n
            self.pack(self.outgoing, dest, tiles, table, start, size)
        def send(i):
            self.copy(self.shift(i), self.boson, start, size).start()
        pack(0)
        def one(i):
            pack(i)
            send(i - 1)
        loop(1, self.n - 1, one)
        return lambda: send(self.n - 2)

    def keep(self, tiles, table):
        self.pack(self.incoming, self.boson, tiles, table, 0, self.capacity)

    def received(self):
        loop(1, self.n, lambda s: self.copy(s, (self.boson + self.n - s) % self.n).wait_recv())

    def sent(self):
        loop(1, self.n, lambda s: self.copy(s, self.boson).wait_send())


def greet(block_peers, boson_peers):
    barrier = pltpu.get_barrier_semaphore()
    boson, block = lax.axis_index("boson"), lax.axis_index("block")
    for peer in block_peers:
        pl.semaphore_signal(barrier, inc=1, device_id=(boson, peer), device_id_type=MESH)
    for peer in boson_peers:
        pl.semaphore_signal(barrier, inc=1, device_id=(peer, block), device_id_type=MESH)
    pl.semaphore_wait(barrier, len(block_peers) + len(boson_peers))


def bits(count):
    return count.bit_length() - 1


class Items:
    def __init__(self, nboson, targets, first_row, row_tiles):
        _, col_blocks, count = targets.shape
        points, per_point = count // nboson, row_tiles * col_blocks
        self.total, self.chunks, self.pair = points * per_point, points * PARTS, col_blocks // PARTS
        self.row_tiles = row_tiles
        boson = lax.axis_index("boson")
        flat = targets[pl.ds(first_row, row_tiles)].reshape(per_point, count)
        lane = lax.broadcasted_iota(jnp.int32, flat.shape, 1)
        own = jnp.concatenate(
            [jnp.sum(jnp.where(lane == boson * points + q, flat, 0), axis=1, keepdims=True)
             for q in range(points)], axis=0)
        self.item = lax.broadcasted_iota(jnp.int32, (self.total, 1), 0)
        self.shift = ((own >> bits(points)) - boson) & (nboson - 1)
        self.row = (self.item >> bits(col_blocks)) & (row_tiles - 1)
        self.column = self.item & (col_blocks - 1)
        self.target = (own & (points - 1)) * per_point + (self.item & (per_point - 1))
        part = self.column >> bits(self.pair)
        self.ahead = (self.item >> bits(per_point)) * PARTS + part
        self.home = (own & (points - 1)) * PARTS + part

    def spread(self, keys, values, width):
        wanted = lax.broadcasted_iota(jnp.int32, (self.total, width), 1)
        return jnp.sum(jnp.where(keys == wanted, values, 0), axis=0, keepdims=True)

    def tile(self, chunk, places):
        if places is not None:
            lane = lax.broadcasted_iota(jnp.int32, (self.total, places.shape[1]), 1)
            chunk = jnp.sum(jnp.where(chunk == lane, places, 0), axis=1, keepdims=True)
        return (chunk * self.row_tiles + self.row) * self.pair + (self.column & (self.pair - 1))


def slot_tables(nboson, capacity, items, ahead_places, home_places, rows):
    boson = lax.axis_index("boson")
    same = items.spread(items.item, items.shift, items.total) == items.shift
    def rank(key):
        later = same & (items.spread(items.item, key, items.total) > key)
        return capacity - 1 - jnp.sum(jnp.where(later, 1, 0), axis=1, keepdims=True)

    there = ((boson + items.shift) & (nboson - 1)) * capacity
    here = ((boson - items.shift) & (nboson - 1)) * capacity
    ahead = items.tile(items.ahead, ahead_places)
    home = items.tile(items.home, home_places)
    out_rank, back_rank = rank(ahead), rank(home)
    width = rows.shape[0] // 8 * rows.shape[1]
    last_slot, last_item = nboson * capacity - 1, items.total - 1
    for k, (keys, values, last) in enumerate((
            (items.item, there + back_rank, last_slot), (there + out_rank, ahead, last_item),
            (items.target, here + out_rank, last_slot), (here + back_rank, home, last_item))):
        line = jnp.clip(items.spread(keys, values, width), 0, last)
        for h in range(width // LANES):
            rows[h * 8 + k:h * 8 + k + 1, :] = line[:, h * LANES:(h + 1) * LANES]


def choose_orders(nboson, nblock, capacity, fixed, lag, targets, row_tiles, rows):
    def counts(pick, items_of):
        total = 0.
        for b, items in enumerate(items_of):
            lane = lax.broadcasted_iota(jnp.int32, (items.total, LANES), 1)
            hot = jnp.where(lane == b * nboson + items.shift, 1., 0.).astype(jnp.bfloat16)
            chunk = items.spread(items.item, pick(items), items.total)
            turn = lax.broadcasted_iota(jnp.int32, (items.chunks, items.total), 0)
            member = jnp.where(chunk == turn, 1., 0.).astype(jnp.bfloat16)
            total = total + jnp.dot(member, hot, preferred_element_type=jnp.float32)
        return total

    items_of = [Items(nboson, targets, b * row_tiles, row_tiles) for b in range(nblock)]
    chunks = items_of[0].chunks
    lane = lax.broadcasted_iota(jnp.int32, (1, LANES), 1)
    weighed = (lane < nboson * nblock) & ((lane & (nboson - 1)) > 0)
    chunk = lax.broadcasted_iota(jnp.int32, (chunks, 1), 0)
    tables, begin = [], []
    for pick in (lambda i: i.ahead, lambda i: i.home):
        count = counts(pick, items_of)
        gain = jnp.exp(-jnp.minimum(count, 60.))
        spare = capacity - jnp.sum(count, axis=0, keepdims=True)
        held = jnp.sum(jnp.where(chunk < fixed, count, 0.), axis=0, keepdims=True)
        tables.append((count, gain, spare))
        begin.append((jnp.where(weighed, jnp.exp(jnp.clip(-spare - held, -60., 60.)), 0.),
                      jnp.broadcast_to(jnp.where(chunk < fixed, chunk, -1), (chunks, LANES))))

    def choose(t, state):
        out = []
        for (weight, turn), (_, gain, _) in zip(state, tables):
            score = jnp.sum(weight * gain, axis=1, keepdims=True)
            score = jnp.where(turn < 0, score, jnp.inf)
            best = jnp.min(score, axis=0, keepdims=True)
            index = lax.broadcasted_iota(jnp.int32, score.shape, 0)
            hit = index == jnp.min(jnp.where(score == best, index, chunks), axis=0, keepdims=True)
            weight = weight * jnp.sum(jnp.where(hit, gain, 0.), axis=0, keepdims=True)
            out.append((weight, jnp.where(hit, t, turn)))
        return tuple(out)

    chosen = lax.fori_loop(fixed, chunks, choose, tuple(begin))
    late = jnp.zeros((1, LANES), jnp.float32)
    turns = []
    for k, ((_, turn), (count, _, spare)) in enumerate(zip(chosen, tables)):
        index = lax.broadcasted_iota(jnp.int32, turn.shape, 0)
        column = lax.broadcasted_iota(jnp.int32, turn.shape, 1)
        order = jnp.sum(jnp.where(turn == column, index, 0), axis=0, keepdims=True)
        rows[k:k + 1, :] = jnp.clip(order, 0, chunks - 1)
        turned = jnp.sum(jnp.where(index == column, turn, 0), axis=0, keepdims=True)
        turns.append(jnp.clip(turned, 0, chunks - 1))
        rows[k + 2:k + 3, :] = turns[k]
        for g in range(lag, chunks):
            ready = jnp.sum(jnp.where(turn <= g, count, 0.), axis=0, keepdims=True)
            late = late + jnp.where(weighed & (ready + spare < g + 1 - lag), 1., 0.)
    return turns, jnp.sum(late, axis=1, keepdims=True)


class Table:
    def __init__(self, ref, k):
        self.ref, self.k = ref, k

    def __getitem__(self, i):
        return self.ref[i // LANES * 8 + self.k, i % LANES]


def kernel(nboson, nblock, row_tiles, col_blocks, lag, *refs):
    relabel, gamma_in, full_in, chi_ph, pp_in, chi_pp, out, *refs = refs
    early = lag is not None
    late, refs = (refs[0], refs[1:]) if early else (None, refs)
    (full, pp, full_blocks, pp_blocks, gamma, scaled, base, tiles, packed, landed, back, returned,
     targets, table_rows, table, order_rows, orders,
     gamma_sem, table_sem, ahead_s, ahead_r, home_s, home_r, *gather_sems) = refs
    half = len(gather_sems) // 2
    chunks = full.shape[0]
    fixed = FIXED if early else chunks
    first = Gather(nblock, full_in, full_blocks, full, fixed, gather_sems[:half])
    second = Gather(nblock, pp_in, pp_blocks, pp, fixed, gather_sems[half:])
    ahead = Exchange(nboson, packed, landed, ahead_s, ahead_r)
    home = Exchange(nboson, back, returned, home_s, home_r)
    points, rows, order = gamma.shape
    high, wide = rows // row_tiles, order // col_blocks
    pair = first.cols // wide
    capacity = landed.shape[1]
    send_slot, item_of, back_slot, back_item_of = (Table(table, i) for i in range(4))
    load_targets = pltpu.make_async_copy(relabel, targets, table_sem.at[0])
    load_table = pltpu.make_async_copy(table_rows, table, table_sem.at[1])
    load_gamma = pltpu.make_async_copy(gamma_in, gamma, gamma_sem)

    load_targets.start()
    for g in range(chunks):
        first.load(g).start()
    load_gamma.start()
    for g in range(chunks):
        second.load(g).start()
    greet(first.peers(), ahead.peers())
    for g in range(fixed):
        first.load(g).wait()
    first.start(0, fixed)

    load_targets.wait()
    if early:
        turns, count = choose_orders(
            nboson, nblock, capacity, fixed, lag, targets, row_tiles, order_rows)
        load_orders = pltpu.make_async_copy(order_rows, orders, table_sem.at[2])
        load_orders.start()
        late[...] = jnp.broadcast_to(count, late.shape)
        for g in range(fixed, chunks):
            first.load(g).wait()
        load_orders.wait()
        first.pack(lambda g: orders[0, g])
    else:
        turns = None, None

    items = Items(nboson, targets, lax.axis_index("block") * row_tiles, row_tiles)
    slot_tables(nboson, capacity, items, *turns, table_rows)
    if early:
        first.start(fixed, chunks)
    load_table.start()
    load_gamma.wait()
    for q in range(points):
        scaled[q] = (gamma[q].astype(jnp.float32) * chi_ph[q:q + 1, :]).astype(jnp.bfloat16)
    load_table.wait()

    def product(gather, g, k):
        point = (orders[k, g] if early else g) // PARTS
        phi = jnp.dot(scaled[point], gather.whole[g], preferred_element_type=jnp.float32)
        wire = phi.astype(jnp.bfloat16)
        for r in range(row_tiles):
            for i in range(pair):
                tiles[(g * row_tiles + r) * pair + i] = (
                    wire[r * high:(r + 1) * high, i * wide:(i + 1) * wide])
        return phi

    def staged(exchange, table, step):
        begin = lag if early else chunks
        loop(0, begin, step)
        def one(g):
            step(g)
            exchange.part(tiles, table, g - begin, 1)()
        loop(begin, chunks, one)
        last = exchange.part(tiles, table, chunks - begin, capacity - (chunks - begin))
        exchange.keep(tiles, table)
        last()

    def ahead_step(g):
        first.relay(g)
        @pl.when(g == chunks - 2)
        def _():
            for i in range(chunks):
                second.load(i).wait()
            if early:
                second.pack(lambda i: orders[1, i])
        @pl.when(g == chunks - 1)
        def _():
            second.start(0, chunks)
        first.arrived(g)
        base[g] = product(first, g, 0)

    staged(ahead, item_of, ahead_step)
    first.sent()
    waiting = chunks // 4
    loop(0, waiting, second.relay)
    ahead.received()

    flat = landed.reshape(nboson * capacity, high, wide)
    def unpack(p):
        chi = chi_pp[pl.ds(p, 1), :]
        for c in range(col_blocks):
            for r in range(row_tiles):
                tile = flat[back_slot[(p * row_tiles + r) * col_blocks + c]]
                scaled[p, r * high:(r + 1) * high, c * wide:(c + 1) * wide] = (
                    tile.astype(jnp.float32) * chi[:, c * wide:(c + 1) * wide]).astype(jnp.bfloat16)
    loop(0, points, unpack)

    def home_step(g):
        @pl.when(g >= waiting)
        def _():
            second.relay(g)
        second.arrived(g)
        product(second, g, 1)

    staged(home, back_item_of, home_step)
    ahead.sent()
    second.sent()
    home.received()

    flat_back = returned.reshape(nboson * capacity, high, wide)
    def finish(q):
        for c in range(col_blocks):
            chunk = q * PARTS + c // pair
            turn = orders[2, chunk] if early else chunk
            for r in range(row_tiles):
                tile = flat_back[send_slot[(q * row_tiles + r) * col_blocks + c]]
                at = (q, slice(r * high, (r + 1) * high), slice(c * wide, (c + 1) * wide))
                phi = base[turn, r * high:(r + 1) * high, c % pair * wide:(c % pair + 1) * wide]
                total = gamma[at].astype(jnp.float32) + phi + tile.astype(jnp.float32)
                out[at] = total.astype(jnp.bfloat16)
    loop(0, points, finish)
    home.sent()


def local(nboson, nblock, gamma_ph, full_ph, chi_ph, pp_vertex, chi_pp, relabel):
    points, rows, order = gamma_ph.shape
    row_tiles, col_blocks = relabel.shape[1] // nblock, relabel.shape[2]
    high, wide = rows // row_tiles, order // col_blocks
    total = points * row_tiles * col_blocks
    capacity = -(-total // nboson) + 1
    bf16, f32 = jnp.bfloat16, jnp.float32
    chunks, cols = points * PARTS, order // PARTS
    whole = pltpu.VMEM((chunks, order, cols), bf16)
    blocks = pltpu.VMEM((chunks, rows, cols), bf16)
    shard = pltpu.VMEM(gamma_ph.shape, bf16)
    slabs = pltpu.VMEM((nboson, capacity, high, wide), bf16)
    table_rows = -(-(nboson * capacity) // LANES) * 8
    for count in (nboson, points, row_tiles * col_blocks, col_blocks, PARTS):
        assert count & (count - 1) == 0
    vmem = pl.BlockSpec(memory_space=pltpu.VMEM)
    hbm = pl.BlockSpec(memory_space=pl.ANY)
    operands = (relabel.transpose(1, 2, 0), gamma_ph, full_ph, chi_ph, pp_vertex, chi_pp)

    def window(lag):
        result = pltpu.VMEM(gamma_ph.shape, bf16)
        early = lag is not None
        return pl.pallas_call(
            functools.partial(kernel, nboson, nblock, row_tiles, col_blocks, lag),
            out_shape=(result, pltpu.VMEM((8, LANES), jnp.float32)) if early else result,
            name="early" if early else "plain",
            in_specs=[hbm, hbm, hbm, vmem, hbm, vmem], out_specs=(vmem, vmem) if early else vmem,
            scratch_shapes=[
                whole, whole, blocks, blocks, shard, shard, pltpu.VMEM((chunks, rows, cols), f32),
                pltpu.VMEM((total, high, wide), bf16), slabs, slabs, slabs, slabs,
                pltpu.VMEM(operands[0].shape, jnp.int32),
                pltpu.VMEM((table_rows, LANES), jnp.int32), pltpu.SMEM((table_rows, LANES), jnp.int32),
                pltpu.VMEM((8, LANES), jnp.int32), pltpu.SMEM((8, LANES), jnp.int32),
                DMA, DMA((3,)), DMA((nboson,)), DMA((nboson,)), DMA((nboson,)), DMA((nboson,)),
            ] + gather_scratch(nblock, points) + gather_scratch(nblock, points),
            compiler_params=pltpu.CompilerParams(
                collective_id=int(early), has_side_effects=True, vmem_limit_bytes=60 * 1024 * 1024),
        )(*operands)

    if capacity <= chunks - LAG or nboson * nblock > LANES:
        return window(None)
    result, late = window(LAG)
    return lax.cond(late[0, 0] == 0, lambda: result, lambda: window(None))


def solution(mesh):
    placed = (
        P("boson", "block", None),
        P("boson", "block", None),
        P("boson", None),
        P("boson", "block", None),
        P("boson", None),
        P(),
    )
    return jax.shard_map(
        functools.partial(local, mesh.shape["boson"], mesh.shape["block"]), mesh=mesh,
        in_specs=placed, out_specs=P("boson", "block", None), check_vma=False,
    )
```

time: 135 us -> 127 us (0.941)
  Pallas kernels: 132 us -> 124 us
    pallas_call x1, Pallas kernels: 132 us -> 124 us  [window(): pl.pallas_call(functools.partial(kernel, nboson, nblock, row_tiles, col_b...]
where the time goes in v1:
time: 127 us; the launch traced here: 126 us
  Pallas kernels  124 us (98%)
  local copies, waits for them, and re-layouts  1.85 us (1%)
    pallas_call x1, Pallas kernels, window(): pl.pallas_call(functools.partial(kernel, nboson, nblock, row_tiles, col_b...  124 us

profile of v1, /device:TPU:10, one launch (start us, length us, event | category | flops | bytes accessed | tf_op | source)
XLA Modules:
  0.0 126.2 jit_solution(13030105374500980480)
XLA Ops:
  0.0 0.0 copy-start
  0.0 0.0 copy-start.1
  0.0 0.0 copy-start.2
  0.0 123.6 %early.1 = (bf16[4,256,1024]{2,1,0:T(8,128)(2,1)S(1)}, f32[8,128]{1,0:T(8,128)S(1)}) custom-call(s32[16,8,32]{2,1,0:T(8,128)} %bitcast.2, bf16[4,256,1024]{2,1,0:T(8,128)(2,1)} %refs_1_.1, bf16[4,256,1024]{2,1,0:T(8,128)(2,1)} %refs_2_.1, f32[4,1024]{1,0:T(4,128)} %refs_3_.1, bf16[4,256,1024]{2,1,0:T(8,128)(2,1)} %refs_4_.1, f32[4,1024]{1,0:T(4,128)} %refs_5_.1), custom_call_target="tpu_custom_call" | custom-call | tf_op jit(solution)/shard_map/early/pallas_call | solution.py:450
  123.6 0.5 slice.3
  124.8 0.0 copy-done
  124.8 0.0 copy-done.1
  124.8 0.0 copy-done.2
  124.9 1.3 %copy.12 = bf16[4,256,1024]{2,1,0:T(8,128)(2,1)} copy(bf16[4,256,1024]{2,1,0:T(8,128)(2,1)S(1)} %get-tuple-element.31) | data formatting | bytes 4194304
  (1 shorter events, 0.0 us)
Async XLA Ops:
  0.0 124.8 %copy-start = (s32[32,16,8]{0,2,1:T(8,128)S(1)}, s32[32,16,8]{0,2,1:T(8,128)}, u32[]{:S(2)}) copy-start(s32[32,16,8]{0,2,1:T(8,128)} %param.13) | copy-start | bytes 49156
  0.0 124.8 %copy-start.1 = (f32[4,1024]{1,0:T(4,128)S(1)}, f32[4,1024]{1,0:T(4,128)}, u32[]{:S(2)}) copy-start(f32[4,1024]{1,0:T(4,128)} %refs_3_.1) | copy-start | bytes 49156
  0.0 124.8 %copy-start.2 = (f32[4,1024]{1,0:T(4,128)S(1)}, f32[4,1024]{1,0:T(4,128)}, u32[]{:S(2)}) copy-start(f32[4,1024]{1,0:T(4,128)} %refs_5_.1) | copy-start | bytes 49156

commit v2 on v1

--- a/solution.py
+++ b/solution.py
@@ -10,7 +10,7 @@
 DMA = pltpu.SemaphoreType.DMA
 PARTS = 4
 FIXED = 2
-LAG = 3
+LAG = 2
 LANES = 128
 
 
@@ -71,11 +71,11 @@
         for j in range(1, self.nblock // 2):
             act(j)
 
-    def start(self, begin, end):
-        def one(g):
-            self.each_far(lambda j: self.far(g, j, self.here).start())
-            self.near(g, self.here).start()
-        loop(begin, end, one)
+    def start_far(self, begin, end):
+        loop(begin, end, lambda g: self.each_far(lambda j: self.far(g, j, self.here).start()))
+
+    def start_near(self, begin, end):
+        loop(begin, end, lambda g: self.near(g, self.here).start())
 
     def relay(self, g):
         def one(j):
@@ -91,9 +91,12 @@
             self.forward(g, j, twin).wait_recv()
         self.each_far(one)
 
-    def sent(self):
+    def left(self, g):
+        self.each_far(lambda j: self.far(g, j, self.here).wait_send())
+
+    def sent(self, begin, end):
+        loop(begin, end, self.left)
         def one(g):
-            self.each_far(lambda j: self.far(g, j, self.here).wait_send())
             self.near(g, self.here).wait_send()
             def fwd(j):
                 owner = (self.here + self.nblock - 2 * j) % self.nblock
@@ -134,18 +137,26 @@
         for k in range(size):
             target[dest, start + k] = tiles[table[dest * self.capacity + start + k]]
 
-    def part(self, tiles, table, start, size):
-        def pack(i):
+    def part(self, tiles, table, start, size, first=False, last=False):
+        behind = (start if first else start - 1, size - first + last)
+        def pack(i, slots):
             dest = (self.boson + self.shift(i)) % self.n
-            self.pack(self.outgoing, dest, tiles, table, start, size)
-        def send(i):
-            self.copy(self.shift(i), self.boson, start, size).start()
-        pack(0)
+            self.pack(self.outgoing, dest, tiles, table, *slots)
+        def send(i, slots):
+            self.copy(self.shift(i), self.boson, *slots).start()
+        now = (start, size)
+        pack(0, now)
         def one(i):
-            pack(i)
-            send(i - 1)
-        loop(1, self.n - 1, one)
-        return lambda: send(self.n - 2)
+            pack(i, now)
+            send(i - 1, now)
+        loop(1, self.n - 3, one)
+        waiting = functools.partial(send, self.n - 4, now)
+        if behind[1] > 0:
+            for i in (self.n - 3, self.n - 2):
+                pack(i, behind)
+                waiting()
+                waiting = functools.partial(send, i, behind)
+        return waiting
 
     def keep(self, tiles, table):
         self.pack(self.incoming, self.boson, tiles, table, 0, self.capacity)
@@ -157,14 +168,35 @@
         loop(1, self.n, lambda s: self.copy(s, self.boson).wait_send())
 
 
-def greet(block_peers, boson_peers):
-    barrier = pltpu.get_barrier_semaphore()
-    boson, block = lax.axis_index("boson"), lax.axis_index("block")
-    for peer in block_peers:
-        pl.semaphore_signal(barrier, inc=1, device_id=(boson, peer), device_id_type=MESH)
-    for peer in boson_peers:
-        pl.semaphore_signal(barrier, inc=1, device_id=(peer, block), device_id_type=MESH)
-    pl.semaphore_wait(barrier, len(block_peers) + len(boson_peers))
+class Greeting:
+    def __init__(self, block_peers, boson_peers):
+        self.barrier = pltpu.get_barrier_semaphore()
+        boson, block = lax.axis_index("boson"), lax.axis_index("block")
+        self.peers = [(boson, peer) for peer in block_peers] + [(peer, block) for peer in boson_peers]
+
+    def say(self):
+        for peer in self.peers:
+            pl.semaphore_signal(self.barrier, inc=1, device_id=peer, device_id_type=MESH)
+
+    def hear(self):
+        pl.semaphore_wait(self.barrier, len(self.peers))
+
+
+class Plan:
+    def __init__(self, *runs):
+        self.runs = runs
+
+    def due(self):
+        chunk = slot = 0
+        for times, chunks, slots in self.runs:
+            for _ in range(times):
+                chunk, slot = chunk + chunks, slot + slots
+                yield chunk, slot
+
+
+def plans(chunks, lag):
+    ahead = Plan((1, lag + 1, 1), (chunks - lag - 1, 1, 1))
+    return ahead, Plan((1, lag + 1, 1), ((chunks - lag - 2) // 2, 2, 2))
 
 
 def bits(count):
@@ -225,7 +257,7 @@
             rows[h * 8 + k:h * 8 + k + 1, :] = line[:, h * LANES:(h + 1) * LANES]
 
 
-def choose_orders(nboson, nblock, capacity, fixed, lag, targets, row_tiles, rows):
+def choose_orders(nboson, nblock, capacity, fixed, plans, targets, row_tiles, rows):
     def counts(pick, items_of):
         total = 0.
         for b, items in enumerate(items_of):
@@ -242,19 +274,24 @@
     lane = lax.broadcasted_iota(jnp.int32, (1, LANES), 1)
     weighed = (lane < nboson * nblock) & ((lane & (nboson - 1)) > 0)
     chunk = lax.broadcasted_iota(jnp.int32, (chunks, 1), 0)
+    shift = lane & (nboson - 1)
+    behind = jnp.where((shift == 1) | (shift == nboson - 1), 1., 0.)
     tables, begin = [], []
-    for pick in (lambda i: i.ahead, lambda i: i.home):
+    for pick, held in zip((lambda i: i.ahead, lambda i: i.home), fixed):
         count = counts(pick, items_of)
-        gain = jnp.exp(-jnp.minimum(count, 60.))
-        spare = capacity - jnp.sum(count, axis=0, keepdims=True)
-        held = jnp.sum(jnp.where(chunk < fixed, count, 0.), axis=0, keepdims=True)
+        gain = jnp.exp(-2. * jnp.minimum(count, 30.))
+        spare = capacity - jnp.sum(count, axis=0, keepdims=True) + behind
+        ready = spare + jnp.sum(jnp.where(chunk < held, count, 0.), axis=0, keepdims=True)
         tables.append((count, gain, spare))
-        begin.append((jnp.where(weighed, jnp.exp(jnp.clip(-spare - held, -60., 60.)), 0.),
-                      jnp.broadcast_to(jnp.where(chunk < fixed, chunk, -1), (chunks, LANES))))
-
-    def choose(t, state):
+        begin.append((jnp.where(weighed, jnp.exp(-2. * jnp.clip(ready, -30., 30.)), 0.),
+                      jnp.broadcast_to(jnp.where(chunk < held, chunk, -1), (chunks, LANES))))
+
+    def choose(t, state, held=(0, 0)):
         out = []
-        for (weight, turn), (_, gain, _) in zip(state, tables):
+        for (weight, turn), (_, gain, _), first in zip(state, tables, held):
+            if isinstance(t, int) and t < first:
+                out.append((weight, turn))
+                continue
             score = jnp.sum(weight * gain, axis=1, keepdims=True)
             score = jnp.where(turn < 0, score, jnp.inf)
             best = jnp.min(score, axis=0, keepdims=True)
@@ -264,10 +301,13 @@
             out.append((weight, jnp.where(hit, t, turn)))
         return tuple(out)
 
-    chosen = lax.fori_loop(fixed, chunks, choose, tuple(begin))
+    state = tuple(begin)
+    for held in range(min(fixed), max(fixed)):
+        state = choose(held, state, fixed)
+    chosen = lax.fori_loop(max(fixed), chunks, choose, state)
     late = jnp.zeros((1, LANES), jnp.float32)
     turns = []
-    for k, ((_, turn), (count, _, spare)) in enumerate(zip(chosen, tables)):
+    for k, ((_, turn), (count, _, spare), plan) in enumerate(zip(chosen, tables, plans)):
         index = lax.broadcasted_iota(jnp.int32, turn.shape, 0)
         column = lax.broadcasted_iota(jnp.int32, turn.shape, 1)
         order = jnp.sum(jnp.where(turn == column, index, 0), axis=0, keepdims=True)
@@ -275,9 +315,9 @@
         turned = jnp.sum(jnp.where(index == column, turn, 0), axis=0, keepdims=True)
         turns.append(jnp.clip(turned, 0, chunks - 1))
         rows[k + 2:k + 3, :] = turns[k]
-        for g in range(lag, chunks):
-            ready = jnp.sum(jnp.where(turn <= g, count, 0.), axis=0, keepdims=True)
-            late = late + jnp.where(weighed & (ready + spare < g + 1 - lag), 1., 0.)
+        for done, slots in plan.due():
+            ready = jnp.sum(jnp.where(turn < done, count, 0.), axis=0, keepdims=True)
+            late = late + jnp.where(weighed & (ready + spare < slots), 1., 0.)
     return turns, jnp.sum(late, axis=1, keepdims=True)
 
 
@@ -298,9 +338,10 @@
      gamma_sem, table_sem, ahead_s, ahead_r, home_s, home_r, *gather_sems) = refs
     half = len(gather_sems) // 2
     chunks = full.shape[0]
-    fixed = FIXED if early else chunks
+    fixed, free = (FIXED, 0) if early else (chunks, chunks)
     first = Gather(nblock, full_in, full_blocks, full, fixed, gather_sems[:half])
-    second = Gather(nblock, pp_in, pp_blocks, pp, fixed, gather_sems[half:])
+    second = Gather(nblock, pp_in, pp_blocks, pp, free, gather_sems[half:])
+    ahead_plan, home_plan = plans(chunks, lag) if early else (Plan(), Plan())
     ahead = Exchange(nboson, packed, landed, ahead_s, ahead_r)
     home = Exchange(nboson, back, returned, home_s, home_r)
     points, rows, order = gamma.shape
@@ -312,21 +353,24 @@
     load_table = pltpu.make_async_copy(table_rows, table, table_sem.at[1])
     load_gamma = pltpu.make_async_copy(gamma_in, gamma, gamma_sem)
 
+    greeting = Greeting(first.peers(), ahead.peers())
+    greeting.say()
     load_targets.start()
-    for g in range(chunks):
+    for g in range(fixed):
         first.load(g).start()
-    load_gamma.start()
-    for g in range(chunks):
-        second.load(g).start()
-    greet(first.peers(), ahead.peers())
+    greeting.hear()
     for g in range(fixed):
         first.load(g).wait()
-    first.start(0, fixed)
-
+    first.start_far(0, fixed)
+    for g in range(fixed, chunks):
+        first.load(g).start()
+    first.start_near(0, fixed)
+    load_gamma.start()
     load_targets.wait()
     if early:
         turns, count = choose_orders(
-            nboson, nblock, capacity, fixed, lag, targets, row_tiles, order_rows)
+            nboson, nblock, capacity, (fixed, free), (ahead_plan, home_plan), targets, row_tiles,
+            order_rows)
         load_orders = pltpu.make_async_copy(order_rows, orders, table_sem.at[2])
         load_orders.start()
         late[...] = jnp.broadcast_to(count, late.shape)
@@ -334,13 +378,16 @@
             first.load(g).wait()
         load_orders.wait()
         first.pack(lambda g: orders[0, g])
+        first.start_far(fixed, chunks)
     else:
         turns = None, None
 
+    for g in range(chunks):
+        second.load(g).start()
     items = Items(nboson, targets, lax.axis_index("block") * row_tiles, row_tiles)
     slot_tables(nboson, capacity, items, *turns, table_rows)
     if early:
-        first.start(fixed, chunks)
+        first.start_near(fixed, chunks)
     load_table.start()
     load_gamma.wait()
     for q in range(points):
@@ -357,20 +404,22 @@
                     wire[r * high:(r + 1) * high, i * wide:(i + 1) * wide])
         return phi
 
-    def staged(exchange, table, step):
-        begin = lag if early else chunks
-        loop(0, begin, step)
-        def one(g):
-            step(g)
-            exchange.part(tiles, table, g - begin, 1)()
-        loop(begin, chunks, one)
-        last = exchange.part(tiles, table, chunks - begin, capacity - (chunks - begin))
+    def staged(exchange, table, plan, step):
+        chunk = slot = 0
+        for times, span, slots in plan.runs:
+            def one(i, chunk=chunk, slot=slot, span=span, slots=slots):
+                begin = chunk + i * span
+                loop(begin, begin + span, step)
+                exchange.part(tiles, table, slot + i * slots, slots, first=slot == 0)()
+            one(0) if times == 1 else loop(0, times, one)
+            chunk, slot = chunk + times * span, slot + times * slots
+        loop(chunk, chunks, step)
+        last = exchange.part(tiles, table, slot, capacity - slot, first=slot == 0, last=True)
         exchange.keep(tiles, table)
         last()
 
     def ahead_step(g):
-        first.relay(g)
-        @pl.when(g == chunks - 2)
+        @pl.when(g == chunks - 3)
         def _():
             for i in range(chunks):
                 second.load(i).wait()
@@ -378,12 +427,15 @@
                 second.pack(lambda i: orders[1, i])
         @pl.when(g == chunks - 1)
         def _():
-            second.start(0, chunks)
+            first.left(chunks - 1)
+            second.start_far(0, chunks)
+        first.relay(g)
         first.arrived(g)
         base[g] = product(first, g, 0)
 
-    staged(ahead, item_of, ahead_step)
-    first.sent()
+    staged(ahead, item_of, ahead_plan, ahead_step)
+    second.start_near(0, chunks)
+    first.sent(0, chunks - 1)
     waiting = chunks // 4
     loop(0, waiting, second.relay)
     ahead.received()
@@ -405,9 +457,9 @@
         second.arrived(g)
         product(second, g, 1)
 
-    staged(home, back_item_of, home_step)
+    staged(home, back_item_of, home_plan, home_step)
     ahead.sent()
-    second.sent()
+    second.sent(0, chunks)
     home.received()
 
     flat_back = returned.reshape(nboson * capacity, high, wide)

time: 127 us -> 124 us (0.976)
  Pallas kernels: 124 us -> 121 us
    pallas_call x1, Pallas kernels: 124 us -> 121 us  [window(): pl.pallas_call(functools.partial(kernel, nboson, nblock, row_tiles, col_b...]
where the time goes in v2:
time: 124 us
  Pallas kernels  121 us (98%)
  local copies, waits for them, and re-layouts  1.85 us (1%)
    pallas_call x1, Pallas kernels, window(): pl.pallas_call(functools.partial(kernel, nboson, nblock, row_tiles, col_b...  121 us

profile of v2, /device:TPU:10, one launch (start us, length us, event | category | flops | bytes accessed | tf_op | source)
XLA Modules:
  0.0 123.5 jit_solution(1931369328175533772)
XLA Ops:
  0.0 0.0 copy-start
  0.0 0.0 copy-start.1
  0.0 0.0 copy-start.2
  0.0 121.0 %early.1 = (bf16[4,256,1024]{2,1,0:T(8,128)(2,1)S(1)}, f32[8,128]{1,0:T(8,128)S(1)}) custom-call(s32[16,8,32]{2,1,0:T(8,128)} %bitcast.2, bf16[4,256,1024]{2,1,0:T(8,128)(2,1)} %refs_1_.1, bf16[4,256,1024]{2,1,0:T(8,128)(2,1)} %refs_2_.1, f32[4,1024]{1,0:T(4,128)} %refs_3_.1, bf16[4,256,1024]{2,1,0:T(8,128)(2,1)} %refs_4_.1, f32[4,1024]{1,0:T(4,128)} %refs_5_.1), custom_call_target="tpu_custom_call" | custom-call | tf_op jit(solution)/shard_map/early/pallas_call | solution.py:502
  121.0 0.5 slice.3
  122.2 0.0 copy-done
  122.2 0.0 copy-done.1
  122.2 0.0 copy-done.2
  122.2 1.3 %copy.12 = bf16[4,256,1024]{2,1,0:T(8,128)(2,1)} copy(bf16[4,256,1024]{2,1,0:T(8,128)(2,1)S(1)} %get-tuple-element.31) | data formatting | bytes 4194304
  (1 shorter events, 0.0 us)
Async XLA Ops:
  0.0 122.2 %copy-start = (s32[32,16,8]{0,2,1:T(8,128)S(1)}, s32[32,16,8]{0,2,1:T(8,128)}, u32[]{:S(2)}) copy-start(s32[32,16,8]{0,2,1:T(8,128)} %param.13) | copy-start | bytes 49156
  0.0 122.2 %copy-start.1 = (f32[4,1024]{1,0:T(4,128)S(1)}, f32[4,1024]{1,0:T(4,128)}, u32[]{:S(2)}) copy-start(f32[4,1024]{1,0:T(4,128)} %refs_3_.1) | copy-start | bytes 49156
  0.0 122.2 %copy-start.2 = (f32[4,1024]{1,0:T(4,128)S(1)}, f32[4,1024]{1,0:T(4,128)}, u32[]{:S(2)}) copy-start(f32[4,1024]{1,0:T(4,128)} %refs_5_.1) | copy-start | bytes 49156

commit v3 on v2

--- a/solution.py
+++ b/solution.py
@@ -118,9 +118,6 @@
         self.capacity = outgoing.shape[1]
         self.boson = lax.axis_index("boson")
         self.block = lax.axis_index("block")
-
-    def peers(self):
-        return [(self.boson + s) % self.n for s in range(1, self.n)]
 
     def shift(self, i):
         return self.n // 2 + (1 - 2 * (i % 2)) * ((i + 1) // 2)
@@ -169,10 +166,12 @@
 
 
 class Greeting:
-    def __init__(self, block_peers, boson_peers):
-        self.barrier = pltpu.get_barrier_semaphore()
+    def __init__(self, nboson, block_peers, met):
+        self.barrier, self.met = pltpu.get_barrier_semaphore(), met
         boson, block = lax.axis_index("boson"), lax.axis_index("block")
-        self.peers = [(boson, peer) for peer in block_peers] + [(peer, block) for peer in boson_peers]
+        self.pairs = [(boson + (1 - 2 * (boson // 2 ** bit % 2)) * 2 ** bit, block)
+                      for bit in range(bits(nboson))]
+        self.peers = [(boson, peer) for peer in block_peers] + self.pairs
 
     def say(self):
         for peer in self.peers:
@@ -180,6 +179,14 @@
 
     def hear(self):
         pl.semaphore_wait(self.barrier, len(self.peers))
+
+    def tell(self, bit):
+        pl.semaphore_signal(self.met.at[bit], inc=1, device_id=self.pairs[bit], device_id_type=MESH)
+
+    def pass_on(self, bit):
+        pl.semaphore_wait(self.met.at[bit], 1)
+        if bit + 1 < len(self.pairs):
+            self.tell(bit + 1)
 
 
 class Plan:
@@ -204,19 +211,19 @@
 
 
 class Items:
-    def __init__(self, nboson, targets, first_row, row_tiles):
+    def __init__(self, nboson, targets, first_row, row_tiles, boson=None):
         _, col_blocks, count = targets.shape
         points, per_point = count // nboson, row_tiles * col_blocks
         self.total, self.chunks, self.pair = points * per_point, points * PARTS, col_blocks // PARTS
         self.row_tiles = row_tiles
-        boson = lax.axis_index("boson")
         flat = targets[pl.ds(first_row, row_tiles)].reshape(per_point, count)
         lane = lax.broadcasted_iota(jnp.int32, flat.shape, 1)
         own = jnp.concatenate(
-            [jnp.sum(jnp.where(lane == boson * points + q, flat, 0), axis=1, keepdims=True)
+            [flat[:, q:q + 1] if boson is None else
+             jnp.sum(jnp.where(lane == boson * points + q, flat, 0), axis=1, keepdims=True)
              for q in range(points)], axis=0)
         self.item = lax.broadcasted_iota(jnp.int32, (self.total, 1), 0)
-        self.shift = ((own >> bits(points)) - boson) & (nboson - 1)
+        self.shift = ((own >> bits(points)) - (0 if boson is None else boson)) & (nboson - 1)
         self.row = (self.item >> bits(col_blocks)) & (row_tiles - 1)
         self.column = self.item & (col_blocks - 1)
         self.target = (own & (points - 1)) * per_point + (self.item & (per_point - 1))
@@ -335,7 +342,7 @@
     late, refs = (refs[0], refs[1:]) if early else (None, refs)
     (full, pp, full_blocks, pp_blocks, gamma, scaled, base, tiles, packed, landed, back, returned,
      targets, table_rows, table, order_rows, orders,
-     gamma_sem, table_sem, ahead_s, ahead_r, home_s, home_r, *gather_sems) = refs
+     gamma_sem, table_sem, met, ahead_s, ahead_r, home_s, home_r, *gather_sems) = refs
     half = len(gather_sems) // 2
     chunks = full.shape[0]
     fixed, free = (FIXED, 0) if early else (chunks, chunks)
@@ -353,7 +360,7 @@
     load_table = pltpu.make_async_copy(table_rows, table, table_sem.at[1])
     load_gamma = pltpu.make_async_copy(gamma_in, gamma, gamma_sem)
 
-    greeting = Greeting(first.peers(), ahead.peers())
+    greeting = Greeting(nboson, first.peers(), met)
     greeting.say()
     load_targets.start()
     for g in range(fixed):
@@ -362,6 +369,7 @@
     for g in range(fixed):
         first.load(g).wait()
     first.start_far(0, fixed)
+    greeting.tell(0)
     for g in range(fixed, chunks):
         first.load(g).start()
     first.start_near(0, fixed)
@@ -373,7 +381,7 @@
             order_rows)
         load_orders = pltpu.make_async_copy(order_rows, orders, table_sem.at[2])
         load_orders.start()
-        late[...] = jnp.broadcast_to(count, late.shape)
+        late[0, 0] = jnp.where(jnp.sum(count) > 0, 1, 0)
         for g in range(fixed, chunks):
             first.load(g).wait()
         load_orders.wait()
@@ -384,11 +392,14 @@
 
     for g in range(chunks):
         second.load(g).start()
-    items = Items(nboson, targets, lax.axis_index("block") * row_tiles, row_tiles)
+    items = Items(nboson, targets, lax.axis_index("block") * row_tiles, row_tiles,
+                  lax.axis_index("boson"))
     slot_tables(nboson, capacity, items, *turns, table_rows)
     if early:
         first.start_near(fixed, chunks)
     load_table.start()
+    for bit in range(bits(nboson)):
+        greeting.pass_on(bit)
     load_gamma.wait()
     for q in range(points):
         scaled[q] = (gamma[q].astype(jnp.float32) * chi_ph[q:q + 1, :]).astype(jnp.bfloat16)
@@ -494,6 +505,7 @@
         assert count & (count - 1) == 0
     vmem = pl.BlockSpec(memory_space=pltpu.VMEM)
     hbm = pl.BlockSpec(memory_space=pl.ANY)
+    smem = pl.BlockSpec(memory_space=pltpu.SMEM)
     operands = (relabel.transpose(1, 2, 0), gamma_ph, full_ph, chi_ph, pp_vertex, chi_pp)
 
     def window(lag):
@@ -501,16 +513,16 @@
         early = lag is not None
         return pl.pallas_call(
             functools.partial(kernel, nboson, nblock, row_tiles, col_blocks, lag),
-            out_shape=(result, pltpu.VMEM((8, LANES), jnp.float32)) if early else result,
+            out_shape=(result, jax.ShapeDtypeStruct((1, 1), jnp.int32)) if early else result,
             name="early" if early else "plain",
-            in_specs=[hbm, hbm, hbm, vmem, hbm, vmem], out_specs=(vmem, vmem) if early else vmem,
+            in_specs=[hbm, hbm, hbm, vmem, hbm, vmem], out_specs=(vmem, smem) if early else vmem,
             scratch_shapes=[
                 whole, whole, blocks, blocks, shard, shard, pltpu.VMEM((chunks, rows, cols), f32),
                 pltpu.VMEM((total, high, wide), bf16), slabs, slabs, slabs, slabs,
                 pltpu.VMEM(operands[0].shape, jnp.int32),
                 pltpu.VMEM((table_rows, LANES), jnp.int32), pltpu.SMEM((table_rows, LANES), jnp.int32),
                 pltpu.VMEM((8, LANES), jnp.int32), pltpu.SMEM((8, LANES), jnp.int32),
-                DMA, DMA((3,)), DMA((nboson,)), DMA((nboson,)), DMA((nboson,)), DMA((nboson,)),
+                DMA, DMA((3,)), pltpu.SemaphoreType.REGULAR((bits(nboson),)), DMA((nboson,)), DMA((nboson,)), DMA((nboson,)), DMA((nboson,)),
             ] + gather_scratch(nblock, points) + gather_scratch(nblock, points),
             compiler_params=pltpu.CompilerParams(
                 collective_id=int(early), has_side_effects=True, vmem_limit_bytes=60 * 1024 * 1024),

time: 124 us -> 123 us (level)
  no operation moved by 1% of the time
where the time goes in v3:
time: 123 us
  Pallas kernels  121 us (98%)
  local copies, waits for them, and re-layouts  1.33 us (1%)
    pallas_call x1, Pallas kernels, window(): pl.pallas_call(functools.partial(kernel, nboson, nblock, row_tiles, col_b...  121 us

profile of v3, /device:TPU:10, one launch (start us, length us, event | category | flops | bytes accessed | tf_op | source)
XLA Modules:
  0.0 123.2 jit_solution(16441003224041788515)
XLA Ops:
  0.0 0.0 copy-start
  0.0 0.0 copy-start.1
  0.0 0.0 copy-start.2
  0.0 121.2 %early.1 = (bf16[4,256,1024]{2,1,0:T(8,128)(2,1)S(1)}, s32[1,1]{1,0:T(1,128)}) custom-call(s32[16,8,32]{2,1,0:T(8,128)} %bitcast.2, bf16[4,256,1024]{2,1,0:T(8,128)(2,1)} %refs_1_.1, bf16[4,256,1024]{2,1,0:T(8,128)(2,1)} %refs_2_.1, f32[4,1024]{1,0:T(4,128)} %refs_3_.1, bf16[4,256,1024]{2,1,0:T(8,128)(2,1)} %refs_4_.1, f32[4,1024]{1,0:T(4,128)} %refs_5_.1), custom_call_target="tpu_custom_call" | custom-call | tf_op jit(solution)/shard_map/early/pallas_call | solution.py:514
  121.8 0.0 copy-done
  121.8 0.0 copy-done.1
  121.8 0.0 copy-done.2
  121.9 1.3 %copy.12 = bf16[4,256,1024]{2,1,0:T(8,128)(2,1)} copy(bf16[4,256,1024]{2,1,0:T(8,128)(2,1)S(1)} %get-tuple-element.31) | data formatting | bytes 4194304
  (1 shorter events, 0.0 us)
Async XLA Ops:
  0.0 121.8 %copy-start = (s32[32,16,8]{0,2,1:T(8,128)S(1)}, s32[32,16,8]{0,2,1:T(8,128)}, u32[]{:S(2)}) copy-start(s32[32,16,8]{0,2,1:T(8,128)} %param.13) | copy-start | bytes 49156
  0.0 121.8 %copy-start.1 = (f32[4,1024]{1,0:T(4,128)S(1)}, f32[4,1024]{1,0:T(4,128)}, u32[]{:S(2)}) copy-start(f32[4,1024]{1,0:T(4,128)} %refs_3_.1) | copy-start | bytes 49156
  0.0 121.8 %copy-start.2 = (f32[4,1024]{1,0:T(4,128)S(1)}, f32[4,1024]{1,0:T(4,128)}, u32[]{:S(2)}) copy-start(f32[4,1024]{1,0:T(4,128)} %refs_5_.1) | copy-start | bytes 49156

commit v4 on v3

--- a/solution.py
+++ b/solution.py
@@ -32,7 +32,7 @@
     def peers(self):
         out = [self.partner]
         for j in range(1, self.nblock // 2):
-            out.append((self.here + 2 * j) % self.nblock)
+            out.append((self.here + 2 * j) & (self.nblock - 1))
         return out
 
     def place(self, g, owner):
@@ -53,7 +53,7 @@
         return pltpu.make_async_remote_copy(
             src_ref=self.place(g, owner), dst_ref=self.place(g, owner),
             send_sem=self.far_s.at[j - 1, g], recv_sem=self.far_r.at[j - 1, g],
-            device_id=(self.boson, (self.here + 2 * j) % self.nblock), device_id_type=MESH)
+            device_id=(self.boson, (self.here + 2 * j) & (self.nblock - 1)), device_id_type=MESH)
 
     def near(self, g, owner):
         return pltpu.make_async_remote_copy(
@@ -79,7 +79,7 @@
 
     def relay(self, g):
         def one(j):
-            owner = (self.here + self.nblock - 2 * j) % self.nblock
+            owner = (self.here + self.nblock - 2 * j) & (self.nblock - 1)
             self.far(g, j, owner).wait_recv()
             self.forward(g, j, owner).start()
         self.each_far(one)
@@ -87,7 +87,7 @@
     def arrived(self, g):
         self.near(g, self.partner).wait_recv()
         def one(j):
-            twin = (self.partner + self.nblock - 2 * j) % self.nblock
+            twin = (self.partner + self.nblock - 2 * j) & (self.nblock - 1)
             self.forward(g, j, twin).wait_recv()
         self.each_far(one)
 
@@ -99,7 +99,7 @@
         def one(g):
             self.near(g, self.here).wait_send()
             def fwd(j):
-                owner = (self.here + self.nblock - 2 * j) % self.nblock
+                owner = (self.here + self.nblock - 2 * j) & (self.nblock - 1)
                 self.forward(g, j, owner).wait_send()
             self.each_far(fwd)
         loop(0, self.chunks, one)
@@ -120,10 +120,10 @@
         self.block = lax.axis_index("block")
 
     def shift(self, i):
-        return self.n // 2 + (1 - 2 * (i % 2)) * ((i + 1) // 2)
+        return self.n // 2 + (1 - 2 * (i & 1)) * ((i + 1) >> 1)
 
     def copy(self, s, slot, start=0, size=None):
-        dest = (self.boson + s) % self.n
+        dest = (self.boson + s) & (self.n - 1)
         slots = pl.ds(start, self.capacity if size is None else size)
         return pltpu.make_async_remote_copy(
             src_ref=self.outgoing.at[dest, slots], dst_ref=self.incoming.at[slot, slots],
@@ -137,7 +137,7 @@
     def part(self, tiles, table, start, size, first=False, last=False):
         behind = (start if first else start - 1, size - first + last)
         def pack(i, slots):
-            dest = (self.boson + self.shift(i)) % self.n
+            dest = (self.boson + self.shift(i)) & (self.n - 1)
             self.pack(self.outgoing, dest, tiles, table, *slots)
         def send(i, slots):
             self.copy(self.shift(i), self.boson, *slots).start()
@@ -159,7 +159,7 @@
         self.pack(self.incoming, self.boson, tiles, table, 0, self.capacity)
 
     def received(self):
-        loop(1, self.n, lambda s: self.copy(s, (self.boson + self.n - s) % self.n).wait_recv())
+        loop(1, self.n, lambda s: self.copy(s, (self.boson + self.n - s) & (self.n - 1)).wait_recv())
 
     def sent(self):
         loop(1, self.n, lambda s: self.copy(s, self.boson).wait_send())
@@ -329,18 +329,20 @@
 
 
 class Table:
-    def __init__(self, ref, k):
-        self.ref, self.k = ref, k
+    def __init__(self, ref, k, size):
+        self.ref, self.k, self.size = ref, k, size
 
     def __getitem__(self, i):
-        return self.ref[i // LANES * 8 + self.k, i % LANES]
+        if self.size <= LANES:
+            return self.ref[self.k, i]
+        return self.ref[(i >> bits(LANES)) * 8 + self.k, i & (LANES - 1)]
 
 
 def kernel(nboson, nblock, row_tiles, col_blocks, lag, *refs):
     relabel, gamma_in, full_in, chi_ph, pp_in, chi_pp, out, *refs = refs
     early = lag is not None
     late, refs = (refs[0], refs[1:]) if early else (None, refs)
-    (full, pp, full_blocks, pp_blocks, gamma, scaled, base, tiles, packed, landed, back, returned,
+    (full, pp, full_blocks, pp_blocks, gamma, scaled, base, sums, tiles, packed, landed, back, returned,
      targets, table_rows, table, order_rows, orders,
      gamma_sem, table_sem, met, ahead_s, ahead_r, home_s, home_r, *gather_sems) = refs
     half = len(gather_sems) // 2
@@ -355,7 +357,9 @@
     high, wide = rows // row_tiles, order // col_blocks
     pair = first.cols // wide
     capacity = landed.shape[1]
-    send_slot, item_of, back_slot, back_item_of = (Table(table, i) for i in range(4))
+    items_here, slots = points * row_tiles * col_blocks, nboson * capacity
+    send_slot, item_of, back_slot, back_item_of = (
+        Table(table, k, size) for k, size in enumerate((items_here, slots, items_here, slots)))
     load_targets = pltpu.make_async_copy(relabel, targets, table_sem.at[0])
     load_table = pltpu.make_async_copy(table_rows, table, table_sem.at[1])
     load_gamma = pltpu.make_async_copy(gamma_in, gamma, gamma_sem)
@@ -390,8 +394,6 @@
     else:
         turns = None, None
 
-    for g in range(chunks):
-        second.load(g).start()
     items = Items(nboson, targets, lax.axis_index("block") * row_tiles, row_tiles,
                   lax.axis_index("boson"))
     slot_tables(nboson, capacity, items, *turns, table_rows)
@@ -400,13 +402,17 @@
     load_table.start()
     for bit in range(bits(nboson)):
         greeting.pass_on(bit)
+    first.relay(0)
     load_gamma.wait()
     for q in range(points):
         scaled[q] = (gamma[q].astype(jnp.float32) * chi_ph[q:q + 1, :]).astype(jnp.bfloat16)
     load_table.wait()
+    for g in range(chunks):
+        second.load(g).start()
+    first.relay(1)
 
     def product(gather, g, k):
-        point = (orders[k, g] if early else g) // PARTS
+        point = (orders[k, g] if early else g) >> bits(PARTS)
         phi = jnp.dot(scaled[point], gather.whole[g], preferred_element_type=jnp.float32)
         wire = phi.astype(jnp.bfloat16)
         for r in range(row_tiles):
@@ -440,7 +446,9 @@
         def _():
             first.left(chunks - 1)
             second.start_far(0, chunks)
-        first.relay(g)
+        @pl.when(g > 1)
+        def _():
+            first.relay(g)
         first.arrived(g)
         base[g] = product(first, g, 0)
 
@@ -469,6 +477,12 @@
         product(second, g, 1)
 
     staged(home, back_item_of, home_plan, home_step)
+    def settle(q):
+        for part in range(PARTS):
+            chunk = q * PARTS + part
+            at = (q, slice(None), slice(part * first.cols, (part + 1) * first.cols))
+            sums[at] = gamma[at].astype(jnp.float32) + base[orders[2, chunk] if early else chunk]
+    loop(0, points, settle)
     ahead.sent()
     second.sent(0, chunks)
     home.received()
@@ -476,14 +490,10 @@
     flat_back = returned.reshape(nboson * capacity, high, wide)
     def finish(q):
         for c in range(col_blocks):
-            chunk = q * PARTS + c // pair
-            turn = orders[2, chunk] if early else chunk
             for r in range(row_tiles):
                 tile = flat_back[send_slot[(q * row_tiles + r) * col_blocks + c]]
                 at = (q, slice(r * high, (r + 1) * high), slice(c * wide, (c + 1) * wide))
-                phi = base[turn, r * high:(r + 1) * high, c % pair * wide:(c % pair + 1) * wide]
-                total = gamma[at].astype(jnp.float32) + phi + tile.astype(jnp.float32)
-                out[at] = total.astype(jnp.bfloat16)
+                out[at] = (sums[at] + tile.astype(jnp.float32)).astype(jnp.bfloat16)
     loop(0, points, finish)
     home.sent()
 
@@ -501,7 +511,7 @@
     shard = pltpu.VMEM(gamma_ph.shape, bf16)
     slabs = pltpu.VMEM((nboson, capacity, high, wide), bf16)
     table_rows = -(-(nboson * capacity) // LANES) * 8
-    for count in (nboson, points, row_tiles * col_blocks, col_blocks, PARTS):
+    for count in (nboson, nblock, points, row_tiles * col_blocks, col_blocks, PARTS):
         assert count & (count - 1) == 0
     vmem = pl.BlockSpec(memory_space=pltpu.VMEM)
     hbm = pl.BlockSpec(memory_space=pl.ANY)
@@ -518,6 +528,7 @@
             in_specs=[hbm, hbm, hbm, vmem, hbm, vmem], out_specs=(vmem, smem) if early else vmem,
             scratch_shapes=[
                 whole, whole, blocks, blocks, shard, shard, pltpu.VMEM((chunks, rows, cols), f32),
+                pltpu.VMEM(gamma_ph.shape, f32),
                 pltpu.VMEM((total, high, wide), bf16), slabs, slabs, slabs, slabs,
                 pltpu.VMEM(operands[0].shape, jnp.int32),
                 pltpu.VMEM((table_rows, LANES), jnp.int32), pltpu.SMEM((table_rows, LANES), jnp.int32),

time: 123 us -> 122 us (level)
  no operation moved by 1% of the time
where the time goes in v4:
time: 122 us
  Pallas kernels  120 us (98%)
  local copies, waits for them, and re-layouts  1.33 us (1%)
    pallas_call x1, Pallas kernels, window(): pl.pallas_call(functools.partial(kernel, nboson, nblock, row_tiles, col_b...  120 us

profile of v4, /device:TPU:10, one launch (start us, length us, event | category | flops | bytes accessed | tf_op | source)
XLA Modules:
  0.0 122.0 jit_solution(10693032136272600128)
XLA Ops:
  0.0 0.0 copy-start
  0.0 0.0 copy-start.1
  0.0 0.0 copy-start.2
  0.0 120.0 %early.1 = (bf16[4,256,1024]{2,1,0:T(8,128)(2,1)S(1)}, s32[1,1]{1,0:T(1,128)}) custom-call(s32[16,8,32]{2,1,0:T(8,128)} %bitcast.2, bf16[4,256,1024]{2,1,0:T(8,128)(2,1)} %refs_1_.1, bf16[4,256,1024]{2,1,0:T(8,128)(2,1)} %refs_2_.1, f32[4,1024]{1,0:T(4,128)} %refs_3_.1, bf16[4,256,1024]{2,1,0:T(8,128)(2,1)} %refs_4_.1, f32[4,1024]{1,0:T(4,128)} %refs_5_.1), custom_call_target="tpu_custom_call" | custom-call | tf_op jit(solution)/shard_map/early/pallas_call | solution.py:524
  120.6 0.0 copy-done
  120.6 0.0 copy-done.1
  120.6 0.0 copy-done.2
  120.7 1.3 %copy.12 = bf16[4,256,1024]{2,1,0:T(8,128)(2,1)} copy(bf16[4,256,1024]{2,1,0:T(8,128)(2,1)S(1)} %get-tuple-element.31) | data formatting | bytes 4194304
  (1 shorter events, 0.0 us)
Async XLA Ops:
  0.0 120.6 %copy-start = (s32[32,16,8]{0,2,1:T(8,128)S(1)}, s32[32,16,8]{0,2,1:T(8,128)}, u32[]{:S(2)}) copy-start(s32[32,16,8]{0,2,1:T(8,128)} %param.13) | copy-start | bytes 49156
  0.0 120.6 %copy-start.1 = (f32[4,1024]{1,0:T(4,128)S(1)}, f32[4,1024]{1,0:T(4,128)}, u32[]{:S(2)}) copy-start(f32[4,1024]{1,0:T(4,128)} %refs_3_.1) | copy-start | bytes 49156
  0.0 120.6 %copy-start.2 = (f32[4,1024]{1,0:T(4,128)S(1)}, f32[4,1024]{1,0:T(4,128)}, u32[]{:S(2)}) copy-start(f32[4,1024]{1,0:T(4,128)} %refs_5_.1) | copy-start | bytes 49156

commit v5 on v4

--- a/solution.py
+++ b/solution.py
@@ -146,7 +146,11 @@
         def one(i):
             pack(i, now)
             send(i - 1, now)
-        loop(1, self.n - 3, one)
+        if first and last:
+            loop(1, self.n - 3, one)
+        else:
+            for i in range(1, self.n - 3):
+                one(i)
         waiting = functools.partial(send, self.n - 4, now)
         if behind[1] > 0:
             for i in (self.n - 3, self.n - 2):

time: 122 us -> 122 us (level)
  no operation moved by 1% of the time
where the time goes in v5:
time: 122 us
  Pallas kernels  120 us (98%)
  local copies, waits for them, and re-layouts  1.33 us (1%)
    pallas_call x1, Pallas kernels, window(): pl.pallas_call(functools.partial(kernel, nboson, nblock, row_tiles, col_b...  120 us

profile of v5, /device:TPU:10, one launch (start us, length us, event | category | flops | bytes accessed | tf_op | source)
XLA Modules:
  0.0 121.9 jit_solution(8664642099346299623)
XLA Ops:
  0.0 0.0 copy-start
  0.0 0.0 copy-start.1
  0.0 0.0 copy-start.2
  0.0 119.9 %early.1 = (bf16[4,256,1024]{2,1,0:T(8,128)(2,1)S(1)}, s32[1,1]{1,0:T(1,128)}) custom-call(s32[16,8,32]{2,1,0:T(8,128)} %bitcast.2, bf16[4,256,1024]{2,1,0:T(8,128)(2,1)} %refs_1_.1, bf16[4,256,1024]{2,1,0:T(8,128)(2,1)} %refs_2_.1, f32[4,1024]{1,0:T(4,128)} %refs_3_.1, bf16[4,256,1024]{2,1,0:T(8,128)(2,1)} %refs_4_.1, f32[4,1024]{1,0:T(4,128)} %refs_5_.1), custom_call_target="tpu_custom_call" | custom-call | tf_op jit(solution)/shard_map/early/pallas_call | solution.py:528
  120.5 0.0 copy-done
  120.5 0.0 copy-done.1
  120.5 0.0 copy-done.2
  120.5 1.3 %copy.12 = bf16[4,256,1024]{2,1,0:T(8,128)(2,1)} copy(bf16[4,256,1024]{2,1,0:T(8,128)(2,1)S(1)} %get-tuple-element.31) | data formatting | bytes 4194304
  (1 shorter events, 0.0 us)
Async XLA Ops:
  0.0 120.5 %copy-start = (s32[32,16,8]{0,2,1:T(8,128)S(1)}, s32[32,16,8]{0,2,1:T(8,128)}, u32[]{:S(2)}) copy-start(s32[32,16,8]{0,2,1:T(8,128)} %param.13) | copy-start | bytes 49156
  0.0 120.5 %copy-start.1 = (f32[4,1024]{1,0:T(4,128)S(1)}, f32[4,1024]{1,0:T(4,128)}, u32[]{:S(2)}) copy-start(f32[4,1024]{1,0:T(4,128)} %refs_3_.1) | copy-start | bytes 49156
  0.0 120.5 %copy-start.2 = (f32[4,1024]{1,0:T(4,128)S(1)}, f32[4,1024]{1,0:T(4,128)}, u32[]{:S(2)}) copy-start(f32[4,1024]{1,0:T(4,128)} %refs_5_.1) | copy-start | bytes 49156
